TPU v7x, 32 devices: a whole 2x2x4 slice. The times are simulated.
32 devices in a mesh: ex: 8 (over y, x, core), co: 4 (over z).
Axes of the slice: x: 2, y: 2, z: 4, core: 2. Of those that a mesh axis runs over, the one named last changes fastest.
Arguments:
- train_grads: float32 [8192, 32768], P('ex', 'co')
- queries: float32 [1024, 32768], P('ex', 'co'), may hold values from -6 to 6
- module_ids: int32 [8], replicated, may hold values from 0 to 223
- module_scale: float32 [224], replicated, may hold values from 0.3 to 3
- example_ids: int32 [8192], P('ex'), may hold values from 0 to 8191, as said below
Outputs:
- influence: float32 [1024, 8192], P('co', 'ex')
Inputs may be any that keep to these rules, and one draw needn't show every extreme that they name: `example_ids`: the examples of block s of 1024 rows carry the ids s * 1024 to (s + 1) * 1024 - 1, each once.
All inputs are finite; a program needn't handle non-finite values.
Results may differ from a plain program's by a relative error of at most 0.00008.
Values sent between devices are 32-bit elements; how exact they have to be, the bound alone decides.
A program may use at most 128 MiB of HBM per device.

v0:
```python
import jax
import jax.numpy as jnp
from jax import lax
from jax.sharding import PartitionSpec as P

PROJ = 4096


epsilon = 1e-06


def score_block(query_rows, train_grads):
    return lax.dot_general(
        query_rows,
        train_grads,
        (((1,), (1,)), ((), ())),
        precision=lax.Precision.HIGHEST,
        preferred_element_type=jnp.float32,
    )


def shards(train_grads, queries, module_ids, module_scale, example_ids):
    example_count = train_grads.shape[0]
    coord_count = train_grads.shape[1]
    module_count = module_ids.shape[0]
    offset = lax.axis_index("co") * coord_count
    position = offset + lax.iota(jnp.int32, coord_count)
    table_index = lax.iota(jnp.int32, module_scale.shape[0])
    picked = jnp.sum(
        jnp.where(module_ids[:, None] == table_index[None, :], module_scale[None, :], 0.0), axis=1
    )
    window_index = lax.iota(jnp.int32, module_count)
    local_module = position // PROJ
    coord_scale = jnp.sum(
        jnp.where(local_module[:, None] == window_index[None, :], picked[None, :], 0.0), axis=1
    )
    scaled = queries * coord_scale[None, :]
    squares = jnp.sum(train_grads * train_grads, axis=1)
    norm_total = lax.psum(squares, "co")
    inverse_norm = lax.rsqrt(norm_total + epsilon)
    all_queries = lax.all_gather(scaled, "ex", axis=0, tiled=True)
    own_scores = lax.psum_scatter(
        score_block(all_queries, train_grads), "co", scatter_dimension=0, tiled=True
    )
    normed = own_scores * inverse_norm[None, :]
    local_ids = example_ids - lax.axis_index("ex") * example_count
    return jnp.zeros_like(normed).at[:, local_ids].set(normed)


def solution(mesh):
    return jax.shard_map(
        shards,
        mesh=mesh,
        in_specs=(P("ex", "co"), P("ex", "co"), P(), P(), P("ex")),
        out_specs=P("co", "ex"),
        check_vma=False,
    )
```

profile of v0, /device:TPU:0, one launch (start us, length us, event | category | flops | bytes accessed | tf_op | source)
XLA Modules:
  0.0 382.9 jit_solution(2201664300313711393)
XLA Ops:
  6.5 0.0 all-gather.2.cloned.1.call-start
  6.6 0.9 select_reduce_fusion.1
  7.4 0.1 select_reduce_fusion
  7.6 4.7 %broadcast_multiply_fusion = f32[128,8192]{1,0:T(8,128)} fusion(f32[128,8192]{1,0:T(8,128)} %param.6, f32[8192]{0:T(1024)S(1)} %select_reduce_fusion), kind=kLoop, calls=%fused_computation.2 | loop fusion | flops 1048576 | bytes 8421376 | tf_op jit(solution)/shard_map/mul | solution.py:37
  12.2 0.0 all-gather.2.cloned.1.call-update
  12.3 0.0 reduce-scatter.2.cloned.1.call-start
  12.3 163.5 %all-gather.2.cloned.1.call-done = f32[1024,8192]{1,0:T(8,128)} async-done(((f32[128,8192]{1,0:T(8,128)}), f32[1024,8192]{1,0:T(8,128)}) %all-gather.2.cloned.1.call-update) | async-done | bytes 33554448 | tf_op jit(solution)/shard_map/all_gather | solution.py:41
  175.8 115.0 %fusion.5 = f32[1024,1024]{1,0:T(8,128)} fusion(f32[1024,8192]{1,0:T(8,128)} %all-gather.2.cloned.1.call-done, f32[1024,8192]{1,0:T(8,128)} %param.5), kind=kOutput, calls=%fused_computation.21 | convolution fusion | flops 103079215104 | bytes 71303168 | tf_op jit(solution)/shard_map/dot_general | solution.py:13
  290.8 0.0 copy-start
  290.8 0.0 reduce-scatter.2.cloned.1.call-update
  290.8 12.7 %multiply_reduce_fusion = f32[1024]{0:T(1024)S(1)} fusion(f32[1024,8192]{1,0:T(8,128)} %param.5), kind=kLoop, calls=%fused_computation.1 | loop fusion | flops 16776192 | bytes 33558528 | tf_op jit(solution)/shard_map/reduce_sum | solution.py:38
  303.5 12.3 %psum.7 = f32[1024]{0:T(1024)S(1)} all-reduce(f32[1024]{0:T(1024)S(1)} %multiply_reduce_fusion), channel_id=1, replica_groups=mesh['ex'=8,'co'=4] {'co'}, use_global_device_ids=true, to_apply=%region_4.5 | all-reduce | flops 1024 | bytes 8192 | tf_op jit(solution)/shard_map/psum | solution.py:39
  315.8 0.0 copy-done
  315.9 52.1 %reduce-scatter.2.cloned.1.call-done = f32[256,1024]{1,0:T(8,128)} async-done(((f32[1024,1024]{1,0:T(8,128)}), f32[256,1024]{1,0:T(8,128)}) %reduce-scatter.2.cloned.1.call-update) | async-done | bytes 1048592 | tf_op jit(solution)/shard_map/reduce_scatter | solution.py:42
  368.0 1.3 multiply_bitcast_fusion
  369.3 0.3 copy.8
  369.7 5.0 %scatter_custom_fusion = f32[256,1024]{0,1:T(8,128)S(1)} fusion(s32[1024]{0:T(1024)S(1)} %compare_select_fusion, f32[1024,256]{1,0:T(8,128)S(1)} %copy.8, f32[]{:T(128)} %constant.12.clone.1), kind=kCustom, calls=%fused_computation.4 | custom fusion | bytes 1048580 | tf_op jit(solution)/shard_map/scatter | solution.py:47
  374.7 1.3 copy.9
  (3 shorter events, 0.0 us)
Async XLA Ops:
  6.5 169.3 %all-gather.2.cloned.1.call-start = ((), (), s32[]{:S(2)}) async-start(), calls=%async_computation.1 | async-start | bytes 37748736 | tf_op jit(solution)/shard_map/all_gather | solution.py:41
  12.3 355.7 %reduce-scatter.2.cloned.1.call-start = ((), (), s32[]{:S(2)}) async-start(), calls=%async_computation.2 | async-start | bytes 5242880 | tf_op jit(solution)/shard_map/reduce_scatter | solution.py:42
  290.8 25.1 %copy-start = (s32[1024]{0:T(1024)S(1)}, s32[1024]{0:T(1024)}, u32[]{:S(2)}) copy-start(s32[1024]{0:T(1024)} %param.9) | copy-start | bytes 12292
Sparse Core Ops, SparseCore 0:
  12.4 163.3 all-gather.1
  290.9 77.0 reduce-scatter.1
where the time goes:
time: 383 us
  waiting for transfers between devices  216 us (56%)
  matrix products  115 us (30%)
  other arithmetic  19.8 us (5%)
  between operations  13.5 us (4%)
  blocking collectives  12.3 us (3%)
  local copies, waits for them, and re-layouts  6.69 us (2%)
    all_gather x1, waiting for transfers between devices, shards(): all_queries = lax.all_gather(scaled, 'ex', axis=0, tiled=True)  163 us
    dot_general x1, matrix products, score_block(): lax.dot_general(query_rows, train_grads, (((1,), (1,)), ((), ())), precis...  115 us
    reduce_scatter x1, waiting for transfers between devices, shards(): lax.psum_scatter(score_block(all_queries, train_grads), 'co', scatter_dim...  52.1 us
    reduce_sum x1, other arithmetic, shards(): squares = jnp.sum(train_grads * train_grads, axis=1)  12.7 us
    psum x1, blocking collectives, shards(): norm_total = lax.psum(squares, 'co')  12.3 us
  transfers between devices with their start and end apart: 2, of which 2 were waited for; matrix products, arithmetic and copies ran while one was open for 3% of the time, Pallas kernels for 0%

commit v1 on v0

v1 whole, which is shorter than its diff:
```python
import functools

import jax
import jax.numpy as jnp
from jax import lax
from jax.experimental import pallas as pl
from jax.experimental.pallas import tpu as pltpu
from jax.sharding import PartitionSpec as P

PROJ = 4096
MESH = pl.DeviceIdType.MESH
PIECES = 4
CONTRACT_LAST = (((1,), (1,)), ((), ()))

epsilon = 1e-06


def kernel(n_ex, n_co, pieces, q_ref, g_ref, scale_ref, out_ref, buf,
           ghi, glo, stage, qhi, qlo, part, got, sq_own, sq_got,
           ring_send, ring_recv, sib_send, sib_recv, part_send, part_recv, sq_send, sq_recv, load_sem):
    chips = n_ex // 2
    half = chips // 2
    ex = lax.axis_index("ex")
    co = lax.axis_index("co")
    core = ex % 2

    def snake(pos):
        upper = pos // half
        return pos * (1 - upper) + upper * (half + chips - 1 - pos)

    pos = snake(ex // 2)

    def device_at(step):
        return snake((pos + step + chips) % chips) * 2 + core

    right = device_at(1)
    left = device_at(-1)
    sibling = ex + 1 - 2 * core
    rows = q_ref.shape[0] // pieces
    mid = rows // 2
    width = q_ref.shape[1]
    examples = g_ref.shape[0]
    owned = (n_ex // n_co) * rows

    barrier = pltpu.get_barrier_semaphore()
    for other in (right, left, sibling):
        pl.semaphore_signal(barrier, inc=1, device_id={"ex": other}, device_id_type=MESH)
    for k in range(1, n_co):
        pl.semaphore_signal(barrier, inc=1, device_id={"co": (co + k) % n_co}, device_id_type=MESH)
    pl.semaphore_wait(barrier, 3 + n_co - 1)

    def own_rows(s):
        return q_ref.at[pl.ds(pl.multiple_of(s * rows, rows), rows)]

    def ring_copy(way, d, s, arriving):
        back = d if arriving else d - 1
        origin = device_at(-back if way == 0 else back)
        if d == half and half > 1:
            span = pl.ds(way * mid, mid)
        else:
            span = pl.ds(0, rows)
        if d == 1 and not arriving:
            src = own_rows(s)
        else:
            src = buf.at[s, origin, span]
        return pltpu.make_async_remote_copy(
            src_ref=src,
            dst_ref=buf.at[s, origin, span],
            send_sem=ring_send.at[way, d - 1, s],
            recv_sem=ring_recv.at[way, d - 1, s],
            device_id={"ex": right if way == 0 else left},
            device_id_type=MESH,
        )

    def sibling_copy(off, s, arriving):
        origin = device_at(off)
        if arriving:
            origin = origin + 1 - 2 * core
        src = own_rows(s) if off == 0 and not arriving else buf.at[s, origin]
        return pltpu.make_async_remote_copy(
            src_ref=src,
            dst_ref=buf.at[s, origin],
            send_sem=sib_send.at[off, s],
            recv_sem=sib_recv.at[off, s],
            device_id={"ex": sibling},
            device_id_type=MESH,
        )

    def part_copy(k, s, arriving):
        owner = (co + k) % n_co
        return pltpu.make_async_remote_copy(
            src_ref=part.at[s, pl.ds(pl.multiple_of(owner * owned, owned), owned)],
            dst_ref=got.at[k - 1, s],
            send_sem=part_send.at[k - 1, s],
            recv_sem=part_recv.at[k - 1, s],
            device_id={"co": owner},
            device_id_type=MESH,
        )

    def sq_copy(k):
        return pltpu.make_async_remote_copy(
            src_ref=sq_own,
            dst_ref=sq_got.at[k - 1],
            send_sem=sq_send.at[k - 1],
            recv_sem=sq_recv.at[k - 1],
            device_id={"co": (co + k) % n_co},
            device_id_type=MESH,
        )

    def send_own(s):
        ring_copy(0, 1, s, False).start()
        ring_copy(1, 1, s, False).start()
        sibling_copy(0, s, False).start()

    send_own(0)
    send_own(1)

    tile = stage.shape[0] // 2
    tiles = examples // tile
    strip = min(512, width)

    def g_load(i):
        slot = i % 2
        return pltpu.make_async_copy(
            g_ref.at[pl.ds(pl.multiple_of(i * tile, tile), tile)],
            stage.at[pl.ds(pl.multiple_of(slot * tile, tile), tile)],
            load_sem.at[slot],
        )

    g_load(0).start()

    def split_tile(i, sums):
        @pl.when(i + 1 < tiles)
        def _():
            g_load(i + 1).start()

        g_load(i).wait()
        base = pl.multiple_of((i % 2) * tile, tile)
        dest = pl.multiple_of(i * tile, tile)

        def split_strip(j, total):
            col = pl.ds(pl.multiple_of(j * strip, strip), strip)
            x = stage[pl.ds(base, tile), col]
            hi = x.astype(jnp.bfloat16)
            ghi[pl.ds(dest, tile), col] = hi
            glo[pl.ds(dest, tile), col] = (x - hi.astype(jnp.float32)).astype(jnp.bfloat16)
            xx = x * x
            for lane in range(0, strip, 128):
                total = total + xx[:, lane:lane + 128]
            return total

        total = lax.fori_loop(0, width // strip, split_strip, jnp.zeros((tile, 128), jnp.float32))
        row = jnp.sum(total.T, axis=0, keepdims=True)
        sq_own[:, pl.ds(dest, tile)] = jnp.broadcast_to(row, (8, tile))
        return sums

    lax.fori_loop(0, tiles, split_tile, 0)
    for k in range(1, n_co):
        sq_copy(k).start()

    depth = min(2048, width)
    block = 256
    count = n_ex * rows

    def load(off, side, s):
        origin = device_at(off)
        if side:
            origin = origin + 1 - 2 * core
        src = own_rows(s) if off == 0 and not side else buf.at[s, origin]
        return pltpu.make_async_copy(
            src,
            stage.at[pl.ds(pl.multiple_of(origin * rows, rows), rows)],
            load_sem.at[2 + off * 2 + side],
        )

    def compute(s):
        for off in range(chips):
            load(off, 0, s).start()
        for off in range(chips):
            sibling_copy(off, s, True).wait_recv()
            load(off, 1, s).start()
        for off in range(chips):
            load(off, 0, s).wait()
            load(off, 1, s).wait()

        def split_queries(j, c):
            col = pl.ds(pl.multiple_of(j * strip, strip), strip)
            x = stage[:, col] * scale_ref[:, col]
            hi = x.astype(jnp.bfloat16)
            qhi[:, col] = hi
            qlo[:, col] = (x - hi.astype(jnp.float32)).astype(jnp.bfloat16)
            return c

        lax.fori_loop(0, width // strip, split_queries, 0)

        def block_scores(b, c):
            ex_rows = pl.ds(pl.multiple_of(b * block, block), block)

            def deepen(j, acc):
                col = pl.ds(pl.multiple_of(j * depth, depth), depth)
                a_hi, b_hi = qhi[:, col], ghi[ex_rows, col]
                dot = functools.partial(
                    lax.dot_general, dimension_numbers=CONTRACT_LAST, preferred_element_type=jnp.float32
                )
                small = dot(qlo[:, col], b_hi) + dot(a_hi, glo[ex_rows, col])
                return acc + (small + dot(a_hi, b_hi))

            acc = lax.fori_loop(0, width // depth, deepen, jnp.zeros((count, block), jnp.float32))
            part[s, :, ex_rows] = acc
            return c

        lax.fori_loop(0, examples // block, block_scores, 0)
        for k in range(1, n_co):
            part_copy(k, s, False).start()

    def step(t, c):
        for d in range(1, half + 1):
            s = t - (d - 1)

            @pl.when((s >= 0) & (s < pieces))
            def _():
                ring_copy(0, d, s, True).wait_recv()
                if d < half:
                    ring_copy(0, d + 1, s, False).start()
                ring_copy(1, d, s, True).wait_recv()
                if d < half:
                    ring_copy(1, d + 1, s, False).start()
                if d == 1:
                    @pl.when(s + 2 < pieces)
                    def _():
                        send_own(s + 2)
                sibling_copy(chips - d, s, False).start()
                if d < half:
                    sibling_copy(d, s, False).start()

        s = t - (half - 1)

        @pl.when((s >= 0) & (s < pieces))
        def _():
            compute(s)

        return c

    lax.fori_loop(0, pieces + half - 1, step, 0)

    for k in range(1, n_co):
        sq_copy(k).wait_recv()
    squares = sq_own[...]
    for k in range(1, n_co):
        squares = squares + sq_got[k - 1]
    inverse_norm = lax.rsqrt(squares[0:1] + epsilon)

    def finish(s, c):
        for k in range(1, n_co):
            part_copy(k, s, True).wait_recv()
        total = part[s, pl.ds(pl.multiple_of(co * owned, owned), owned)]
        for k in range(1, n_co):
            total = total + got[k - 1, s]
        total = total * inverse_norm
        for i in range(n_ex // n_co):
            at = pl.multiple_of(i * rows * pieces + s * rows, rows)
            out_ref[pl.ds(at, rows), :] = total[i * rows:(i + 1) * rows]
        return c

    lax.fori_loop(0, pieces, finish, 0)

    def drain(s, c):
        for way in range(2):
            for d in range(1, half + 1):
                ring_copy(way, d, s, False).wait_send()
        for off in range(chips):
            sibling_copy(off, s, False).wait_send()
        for k in range(1, n_co):
            part_copy(k, s, False).wait_send()
        return c

    lax.fori_loop(0, pieces, drain, 0)
    for k in range(1, n_co):
        sq_copy(k).wait_send()


def shards(n_ex, n_co, train_grads, queries, module_ids, module_scale, example_ids):
    examples, width = train_grads.shape
    position = lax.axis_index("co") * width + lax.iota(jnp.int32, width)
    table_index = lax.iota(jnp.int32, module_scale.shape[0])
    picked = jnp.sum(
        jnp.where(module_ids[:, None] == table_index[None, :], module_scale[None, :], 0.0), axis=1
    )
    window_index = lax.iota(jnp.int32, module_ids.shape[0])
    coord_scale = jnp.sum(
        jnp.where((position // PROJ)[:, None] == window_index[None, :], picked[None, :], 0.0), axis=1
    )

    chips = n_ex // 2
    pieces = PIECES
    rows = queries.shape[0] // pieces
    count = n_ex * rows
    owned = (n_ex // n_co) * rows
    f32, bf16 = jnp.float32, jnp.bfloat16
    dma = pltpu.SemaphoreType.DMA
    normed, _ = pl.pallas_call(
        functools.partial(kernel, n_ex, n_co, pieces),
        out_shape=(
            jax.ShapeDtypeStruct((owned * pieces, examples), f32),
            jax.ShapeDtypeStruct((pieces, n_ex, rows, width), f32),
        ),
        in_specs=[
            pl.BlockSpec(memory_space=pl.ANY),
            pl.BlockSpec(memory_space=pl.ANY),
            pl.BlockSpec(memory_space=pltpu.VMEM),
        ],
        out_specs=(pl.BlockSpec(memory_space=pltpu.VMEM), pl.BlockSpec(memory_space=pl.ANY)),
        scratch_shapes=[
            pltpu.VMEM((examples, width), bf16),
            pltpu.VMEM((examples, width), bf16),
            pltpu.VMEM((count, width), f32),
            pltpu.VMEM((count, width), bf16),
            pltpu.VMEM((count, width), bf16),
            pltpu.VMEM((pieces, count, examples), f32),
            pltpu.VMEM((n_co - 1, pieces, owned, examples), f32),
            pltpu.VMEM((8, examples), f32),
            pltpu.VMEM((n_co - 1, 8, examples), f32),
            dma((2, chips // 2, pieces)),
            dma((2, chips // 2, pieces)),
            dma((chips, pieces)),
            dma((chips, pieces)),
            dma((n_co - 1, pieces)),
            dma((n_co - 1, pieces)),
            dma((n_co - 1,)),
            dma((n_co - 1,)),
            dma((2 + n_ex,)),
        ],
        compiler_params=pltpu.CompilerParams(
            collective_id=0, has_side_effects=True, vmem_limit_bytes=67043328
        ),
    )(queries, train_grads, coord_scale[None, :])

    local_ids = example_ids - lax.axis_index("ex") * examples
    place = (local_ids[:, None] == lax.iota(jnp.int32, examples)[None, :]).astype(f32)
    return lax.dot_general(
        normed, place, (((1,), (0,)), ((), ())), precision=lax.Precision.HIGHEST, preferred_element_type=f32
    )


def solution(mesh):
    return jax.shard_map(
        functools.partial(shards, mesh.shape["ex"], mesh.shape["co"]),
        mesh=mesh,
        in_specs=(P("ex", "co"), P("ex", "co"), P(), P(), P("ex")),
        out_specs=P("co", "ex"),
        check_vma=False,
    )
```

time: 383 us -> 208 us (0.54)
  waiting for transfers between devices: 216 us -> 0 us
  Pallas kernels: 0 us -> 198 us
  matrix products: 115 us -> 4.46 us
  other arithmetic: 19.8 us -> 2.35 us
  between operations: 13.5 us -> 0.02 us
  blocking collectives: 12.3 us -> 0 us
  local copies, waits for them, and re-layouts: 6.69 us -> 0 us
    pallas_call x0 -> x1, Pallas kernels: none -> 198 us  [shards(): pl.pallas_call(functools.partial(kernel, n_ex, n_co, pieces), out_shape=(...]
    all_gather x1 -> x0, waiting for transfers between devices: 163 us -> none  [shards(): all_queries = lax.all_gather(scaled, 'ex', axis=0, tiled=True)]
    dot_general x1, matrix products: 115 us -> 4.46 us  [shards(): lax.dot_general(normed, place, (((1,), (0,)), ((), ())), precision=lax.Pr...]
    reduce_scatter x1 -> x0, waiting for transfers between devices: 52.1 us -> none  [shards(): lax.psum_scatter(score_block(all_queries, train_grads), 'co', scatter_dim...]
    psum x1 -> x0, blocking collectives: 12.3 us -> none  [shards(): norm_total = lax.psum(squares, 'co')]
    reduce_sum x2 -> x1, other arithmetic: 12.9 us -> 0.76 us  [shards(): jnp.sum(jnp.where((position // PROJ)[:, None] == window_index[None, :], p...]
    scatter x2 -> x0, local copies, waits for them, and re-layouts: 6.35 us -> none  [shards(): return jnp.zeros_like(normed).at[:, local_ids].set(normed)]
    mul x2 -> x0, other arithmetic: 5.99 us -> none  [the longest x1 4.65 us: shards(): scaled = queries * coord_scale[None, :]]
  transfers between devices with their start and end apart: 2 -> 0, of which waited for: 2 -> 0; matrix products, arithmetic and copies ran while one was open for 3% -> 0% of each run, Pallas kernels for 0% -> 0%
where the time goes in v1:
time: 208 us; the launch traced here: 205 us
  Pallas kernels  198 us (95%)
  matrix products  4.46 us (2%)
  other arithmetic  2.35 us (1%)
    pallas_call x1, Pallas kernels, shards(): pl.pallas_call(functools.partial(kernel, n_ex, n_co, pieces), out_shape=(...  198 us
    dot_general x1, matrix products, shards(): lax.dot_general(normed, place, (((1,), (0,)), ((), ())), precision=lax.Pr...  4.46 us

profile of v1, /device:TPU:0, one launch (start us, length us, event | category | flops | bytes accessed | tf_op | source)
XLA Modules:
  0.0 205.3 jit_solution(3918138163995021554)
XLA Ops:
  0.0 0.9 select_reduce_fusion.1
  0.9 0.8 select_reduce_fusion
  1.7 198.4 %shard_map.55 = (f32[256,1024]{1,0:T(8,128)}, f32[4,8,32,8192]{3,2,1,0:T(8,128)}) custom-call(f32[128,8192]{1,0:T(8,128)} %q_ref.1, f32[1024,8192]{1,0:T(8,128)} %g_ref.1, f32[1,8192]{1,0:T(1,128)} %bitcast.2), custom_call_target="tpu_custom_call" | custom-call | tf_op jit(solution)/shard_map/pallas_call | solution.py:301
  200.1 0.7 broadcast_subtract_fusion
  200.8 4.5 %fusion = f32[256,1024]{1,0:T(8,128)} fusion(f32[256,1024]{1,0:T(8,128)} %get-tuple-element.6, s32[1024]{0:T(1024)S(1)} %broadcast_subtract_fusion), kind=kOutput, calls=%fused_computation.1 | convolution fusion | flops 3222274048 | bytes 2101248 | tf_op jit(solution)/shard_map/dot_general | solution.py:340
  (1 shorter events, 0.0 us)

commit v2 on v1

--- a/solution.py
+++ b/solution.py
@@ -9,14 +9,15 @@
 
 PROJ = 4096
 MESH = pl.DeviceIdType.MESH
-PIECES = 4
+PIECES = 8
+LEAD = 2
 CONTRACT_LAST = (((1,), (1,)), ((), ()))
 
 epsilon = 1e-06
 
 
 def kernel(n_ex, n_co, pieces, q_ref, g_ref, scale_ref, out_ref, buf,
-           ghi, glo, stage, qhi, qlo, part, got, sq_own, sq_got,
+           ghi, glo, fresh, stage, split, part, got, sq_own, sq_got,
            ring_send, ring_recv, sib_send, sib_recv, part_send, part_recv, sq_send, sq_recv, load_sem):
     chips = n_ex // 2
     half = chips // 2
@@ -37,8 +38,8 @@
     left = device_at(-1)
     sibling = ex + 1 - 2 * core
     rows = q_ref.shape[0] // pieces
-    mid = rows // 2
     width = q_ref.shape[1]
+    mid = width // 2
     examples = g_ref.shape[0]
     owned = (n_ex // n_co) * rows
 
@@ -58,14 +59,14 @@
         if d == half and half > 1:
             span = pl.ds(way * mid, mid)
         else:
-            span = pl.ds(0, rows)
+            span = pl.ds(0, width)
         if d == 1 and not arriving:
             src = own_rows(s)
         else:
-            src = buf.at[s, origin, span]
+            src = buf.at[s, origin, :, span]
         return pltpu.make_async_remote_copy(
             src_ref=src,
-            dst_ref=buf.at[s, origin, span],
+            dst_ref=buf.at[s, origin, :, span],
             send_sem=ring_send.at[way, d - 1, s],
             recv_sem=ring_recv.at[way, d - 1, s],
             device_id={"ex": right if way == 0 else left},
@@ -86,13 +87,17 @@
             device_id_type=MESH,
         )
 
-    def part_copy(k, s, arriving):
+    block = 256
+    blocks = examples // block
+
+    def part_copy(k, s, b):
         owner = (co + k) % n_co
+        cols = pl.ds(pl.multiple_of(b * block, block), block)
         return pltpu.make_async_remote_copy(
-            src_ref=part.at[s, pl.ds(pl.multiple_of(owner * owned, owned), owned)],
-            dst_ref=got.at[k - 1, s],
-            send_sem=part_send.at[k - 1, s],
-            recv_sem=part_recv.at[k - 1, s],
+            src_ref=part.at[s, pl.ds(pl.multiple_of(owner * owned, owned), owned), cols],
+            dst_ref=got.at[k - 1, s, :, cols],
+            send_sem=part_send.at[k - 1, s, b],
+            recv_sem=part_recv.at[k - 1, s, b],
             device_id={"co": owner},
             device_id_type=MESH,
         )
@@ -112,10 +117,10 @@
         ring_copy(1, 1, s, False).start()
         sibling_copy(0, s, False).start()
 
-    send_own(0)
-    send_own(1)
-
-    tile = stage.shape[0] // 2
+    for s in range(min(LEAD, pieces)):
+        send_own(s)
+
+    tile = fresh.shape[1]
     tiles = examples // tile
     strip = min(512, width)
 
@@ -123,7 +128,7 @@
         slot = i % 2
         return pltpu.make_async_copy(
             g_ref.at[pl.ds(pl.multiple_of(i * tile, tile), tile)],
-            stage.at[pl.ds(pl.multiple_of(slot * tile, tile), tile)],
+            fresh.at[slot],
             load_sem.at[slot],
         )
 
@@ -135,12 +140,12 @@
             g_load(i + 1).start()
 
         g_load(i).wait()
-        base = pl.multiple_of((i % 2) * tile, tile)
+        slot = i % 2
         dest = pl.multiple_of(i * tile, tile)
 
         def split_strip(j, total):
             col = pl.ds(pl.multiple_of(j * strip, strip), strip)
-            x = stage[pl.ds(base, tile), col]
+            x = fresh[slot, :, col]
             hi = x.astype(jnp.bfloat16)
             ghi[pl.ds(dest, tile), col] = hi
             glo[pl.ds(dest, tile), col] = (x - hi.astype(jnp.float32)).astype(jnp.bfloat16)
@@ -158,8 +163,7 @@
     for k in range(1, n_co):
         sq_copy(k).start()
 
-    depth = min(2048, width)
-    block = 256
+    depth = min(8192, width)
     count = n_ex * rows
 
     def load(off, side, s):
@@ -187,8 +191,8 @@
             col = pl.ds(pl.multiple_of(j * strip, strip), strip)
             x = stage[:, col] * scale_ref[:, col]
             hi = x.astype(jnp.bfloat16)
-            qhi[:, col] = hi
-            qlo[:, col] = (x - hi.astype(jnp.float32)).astype(jnp.bfloat16)
+            split[pl.ds(0, count), col] = hi
+            split[pl.ds(count, count), col] = (x - hi.astype(jnp.float32)).astype(jnp.bfloat16)
             return c
 
         lax.fori_loop(0, width // strip, split_queries, 0)
@@ -198,20 +202,20 @@
 
             def deepen(j, acc):
                 col = pl.ds(pl.multiple_of(j * depth, depth), depth)
-                a_hi, b_hi = qhi[:, col], ghi[ex_rows, col]
                 dot = functools.partial(
                     lax.dot_general, dimension_numbers=CONTRACT_LAST, preferred_element_type=jnp.float32
                 )
-                small = dot(qlo[:, col], b_hi) + dot(a_hi, glo[ex_rows, col])
-                return acc + (small + dot(a_hi, b_hi))
+                both = dot(split[:, col], ghi[ex_rows, col])
+                small = both[count:] + dot(split[:count, col], glo[ex_rows, col])
+                return acc + (small + both[:count])
 
             acc = lax.fori_loop(0, width // depth, deepen, jnp.zeros((count, block), jnp.float32))
             part[s, :, ex_rows] = acc
+            for k in range(1, n_co):
+                part_copy(k, s, b).start()
             return c
 
-        lax.fori_loop(0, examples // block, block_scores, 0)
-        for k in range(1, n_co):
-            part_copy(k, s, False).start()
+        lax.fori_loop(0, blocks, block_scores, 0)
 
     def step(t, c):
         for d in range(1, half + 1):
@@ -226,9 +230,9 @@
                 if d < half:
                     ring_copy(1, d + 1, s, False).start()
                 if d == 1:
-                    @pl.when(s + 2 < pieces)
+                    @pl.when(s + LEAD < pieces)
                     def _():
-                        send_own(s + 2)
+                        send_own(s + LEAD)
                 sibling_copy(chips - d, s, False).start()
                 if d < half:
                     sibling_copy(d, s, False).start()
@@ -252,7 +256,8 @@
 
     def finish(s, c):
         for k in range(1, n_co):
-            part_copy(k, s, True).wait_recv()
+            for b in range(blocks):
+                part_copy(k, s, b).wait_recv()
         total = part[s, pl.ds(pl.multiple_of(co * owned, owned), owned)]
         for k in range(1, n_co):
             total = total + got[k - 1, s]
@@ -271,7 +276,8 @@
         for off in range(chips):
             sibling_copy(off, s, False).wait_send()
         for k in range(1, n_co):
-            part_copy(k, s, False).wait_send()
+            for b in range(blocks):
+                part_copy(k, s, b).wait_send()
         return c
 
     lax.fori_loop(0, pieces, drain, 0)
@@ -292,7 +298,7 @@
     )
 
     chips = n_ex // 2
-    pieces = PIECES
+    pieces = min(PIECES, queries.shape[0] // 8)
     rows = queries.shape[0] // pieces
     count = n_ex * rows
     owned = (n_ex // n_co) * rows
@@ -313,9 +319,9 @@
         scratch_shapes=[
             pltpu.VMEM((examples, width), bf16),
             pltpu.VMEM((examples, width), bf16),
+            pltpu.VMEM((2, min(128, examples), width), f32),
             pltpu.VMEM((count, width), f32),
-            pltpu.VMEM((count, width), bf16),
-            pltpu.VMEM((count, width), bf16),
+            pltpu.VMEM((2 * count, width), bf16),
             pltpu.VMEM((pieces, count, examples), f32),
             pltpu.VMEM((n_co - 1, pieces, owned, examples), f32),
             pltpu.VMEM((8, examples), f32),
@@ -324,8 +330,8 @@
             dma((2, chips // 2, pieces)),
             dma((chips, pieces)),
             dma((chips, pieces)),
-            dma((n_co - 1, pieces)),
-            dma((n_co - 1, pieces)),
+            dma((n_co - 1, pieces, examples // 256)),
+            dma((n_co - 1, pieces, examples // 256)),
             dma((n_co - 1,)),
             dma((n_co - 1,)),
             dma((2 + n_ex,)),

time: 208 us -> 181 us (0.87); the launches traced: 205 us -> 181 us
  Pallas kernels: 198 us -> 174 us
    pallas_call x1, Pallas kernels: 198 us -> 174 us  [shards(): pl.pallas_call(functools.partial(kernel, n_ex, n_co, pieces), out_shape=(...]
where the time goes in v2:
time: 181 us
  Pallas kernels  174 us (96%)
  matrix products  4.46 us (2%)
  other arithmetic  2.35 us (1%)
    pallas_call x1, Pallas kernels, shards(): pl.pallas_call(functools.partial(kernel, n_ex, n_co, pieces), out_shape=(...  174 us
    dot_general x1, matrix products, shards(): lax.dot_general(normed, place, (((1,), (0,)), ((), ())), precision=lax.Pr...  4.46 us

profile of v2, /device:TPU:0, one launch (start us, length us, event | category | flops | bytes accessed | tf_op | source)
XLA Modules:
  0.0 180.7 jit_solution(4328836425135473165)
XLA Ops:
  0.0 0.9 select_reduce_fusion.1
  0.9 0.8 select_reduce_fusion
  1.7 173.8 %shard_map.55 = (f32[256,1024]{1,0:T(8,128)}, f32[8,8,16,8192]{3,2,1,0:T(8,128)}) custom-call(f32[128,8192]{1,0:T(8,128)} %q_ref.1, f32[1024,8192]{1,0:T(8,128)} %g_ref.1, f32[1,8192]{1,0:T(1,128)} %bitcast.2), custom_call_target="tpu_custom_call" | custom-call | tf_op jit(solution)/shard_map/pallas_call | solution.py:307
  175.5 0.7 broadcast_subtract_fusion
  176.2 4.5 %fusion = f32[256,1024]{1,0:T(8,128)} fusion(f32[256,1024]{1,0:T(8,128)} %get-tuple-element.6, s32[1024]{0:T(1024)S(1)} %broadcast_subtract_fusion), kind=kOutput, calls=%fused_computation.1 | convolution fusion | flops 3222274048 | bytes 2101248 | tf_op jit(solution)/shard_map/dot_general | solution.py:346
  (1 shorter events, 0.0 us)

commit v3 on v2

--- a/solution.py
+++ b/solution.py
@@ -120,104 +120,7 @@
     for s in range(min(LEAD, pieces)):
         send_own(s)
 
-    tile = fresh.shape[1]
-    tiles = examples // tile
-    strip = min(512, width)
-
-    def g_load(i):
-        slot = i % 2
-        return pltpu.make_async_copy(
-            g_ref.at[pl.ds(pl.multiple_of(i * tile, tile), tile)],
-            fresh.at[slot],
-            load_sem.at[slot],
-        )
-
-    g_load(0).start()
-
-    def split_tile(i, sums):
-        @pl.when(i + 1 < tiles)
-        def _():
-            g_load(i + 1).start()
-
-        g_load(i).wait()
-        slot = i % 2
-        dest = pl.multiple_of(i * tile, tile)
-
-        def split_strip(j, total):
-            col = pl.ds(pl.multiple_of(j * strip, strip), strip)
-            x = fresh[slot, :, col]
-            hi = x.astype(jnp.bfloat16)
-            ghi[pl.ds(dest, tile), col] = hi
-            glo[pl.ds(dest, tile), col] = (x - hi.astype(jnp.float32)).astype(jnp.bfloat16)
-            xx = x * x
-            for lane in range(0, strip, 128):
-                total = total + xx[:, lane:lane + 128]
-            return total
-
-        total = lax.fori_loop(0, width // strip, split_strip, jnp.zeros((tile, 128), jnp.float32))
-        row = jnp.sum(total.T, axis=0, keepdims=True)
-        sq_own[:, pl.ds(dest, tile)] = jnp.broadcast_to(row, (8, tile))
-        return sums
-
-    lax.fori_loop(0, tiles, split_tile, 0)
-    for k in range(1, n_co):
-        sq_copy(k).start()
-
-    depth = min(8192, width)
-    count = n_ex * rows
-
-    def load(off, side, s):
-        origin = device_at(off)
-        if side:
-            origin = origin + 1 - 2 * core
-        src = own_rows(s) if off == 0 and not side else buf.at[s, origin]
-        return pltpu.make_async_copy(
-            src,
-            stage.at[pl.ds(pl.multiple_of(origin * rows, rows), rows)],
-            load_sem.at[2 + off * 2 + side],
-        )
-
-    def compute(s):
-        for off in range(chips):
-            load(off, 0, s).start()
-        for off in range(chips):
-            sibling_copy(off, s, True).wait_recv()
-            load(off, 1, s).start()
-        for off in range(chips):
-            load(off, 0, s).wait()
-            load(off, 1, s).wait()
-
-        def split_queries(j, c):
-            col = pl.ds(pl.multiple_of(j * strip, strip), strip)
-            x = stage[:, col] * scale_ref[:, col]
-            hi = x.astype(jnp.bfloat16)
-            split[pl.ds(0, count), col] = hi
-            split[pl.ds(count, count), col] = (x - hi.astype(jnp.float32)).astype(jnp.bfloat16)
-            return c
-
-        lax.fori_loop(0, width // strip, split_queries, 0)
-
-        def block_scores(b, c):
-            ex_rows = pl.ds(pl.multiple_of(b * block, block), block)
-
-            def deepen(j, acc):
-                col = pl.ds(pl.multiple_of(j * depth, depth), depth)
-                dot = functools.partial(
-                    lax.dot_general, dimension_numbers=CONTRACT_LAST, preferred_element_type=jnp.float32
-                )
-                both = dot(split[:, col], ghi[ex_rows, col])
-                small = both[count:] + dot(split[:count, col], glo[ex_rows, col])
-                return acc + (small + both[:count])
-
-            acc = lax.fori_loop(0, width // depth, deepen, jnp.zeros((count, block), jnp.float32))
-            part[s, :, ex_rows] = acc
-            for k in range(1, n_co):
-                part_copy(k, s, b).start()
-            return c
-
-        lax.fori_loop(0, blocks, block_scores, 0)
-
-    def step(t, c):
+    def relay(t):
         for d in range(1, half + 1):
             s = t - (d - 1)
 
@@ -236,6 +139,112 @@
                 sibling_copy(chips - d, s, False).start()
                 if d < half:
                     sibling_copy(d, s, False).start()
+
+    tile = fresh.shape[1]
+    tiles = examples // tile
+    strip = min(512, width)
+
+    def g_load(i):
+        slot = i % 2
+        return pltpu.make_async_copy(
+            g_ref.at[pl.ds(pl.multiple_of(i * tile, tile), tile)],
+            fresh.at[slot],
+            load_sem.at[slot],
+        )
+
+    g_load(0).start()
+
+    def split_tile(i, sums):
+        @pl.when(i + 1 < tiles)
+        def _():
+            g_load(i + 1).start()
+
+        @pl.when(i == tiles // 2)
+        def _():
+            relay(0)
+
+        g_load(i).wait()
+        slot = i % 2
+        dest = pl.multiple_of(i * tile, tile)
+
+        def split_strip(j, total):
+            col = pl.ds(pl.multiple_of(j * strip, strip), strip)
+            x = fresh[slot, :, col]
+            hi = x.astype(jnp.bfloat16)
+            ghi[pl.ds(dest, tile), col] = hi
+            glo[pl.ds(dest, tile), col] = (x - hi.astype(jnp.float32)).astype(jnp.bfloat16)
+            xx = x * x
+            for lane in range(0, strip, 128):
+                total = total + xx[:, lane:lane + 128]
+            return total
+
+        total = lax.fori_loop(0, width // strip, split_strip, jnp.zeros((tile, 128), jnp.float32))
+        row = jnp.sum(total.T, axis=0, keepdims=True)
+        sq_own[:, pl.ds(dest, tile)] = jnp.broadcast_to(row, (8, tile))
+        return sums
+
+    lax.fori_loop(0, tiles, split_tile, 0)
+    for k in range(1, n_co):
+        sq_copy(k).start()
+
+    depth = min(8192, width)
+    count = n_ex * rows
+
+    def load(off, side, s):
+        origin = device_at(off)
+        if side:
+            origin = origin + 1 - 2 * core
+        src = own_rows(s) if off == 0 and not side else buf.at[s, origin]
+        return pltpu.make_async_copy(
+            src,
+            stage.at[pl.ds(pl.multiple_of(origin * rows, rows), rows)],
+            load_sem.at[2 + off * 2 + side],
+        )
+
+    def compute(s):
+        for off in range(chips):
+            load(off, 0, s).start()
+        for off in range(chips):
+            sibling_copy(off, s, True).wait_recv()
+            load(off, 1, s).start()
+        for off in range(chips):
+            load(off, 0, s).wait()
+            load(off, 1, s).wait()
+
+        def split_queries(j, c):
+            col = pl.ds(pl.multiple_of(j * strip, strip), strip)
+            x = stage[:, col] * scale_ref[:, col]
+            hi = x.astype(jnp.bfloat16)
+            split[pl.ds(0, count), col] = hi
+            split[pl.ds(count, count), col] = (x - hi.astype(jnp.float32)).astype(jnp.bfloat16)
+            return c
+
+        lax.fori_loop(0, width // strip, split_queries, 0)
+
+        def block_scores(b, c):
+            ex_rows = pl.ds(pl.multiple_of(b * block, block), block)
+
+            def deepen(j, acc):
+                col = pl.ds(pl.multiple_of(j * depth, depth), depth)
+                dot = functools.partial(
+                    lax.dot_general, dimension_numbers=CONTRACT_LAST, preferred_element_type=jnp.float32
+                )
+                both = dot(split[:, col], ghi[ex_rows, col])
+                small = both[count:] + dot(split[:count, col], glo[ex_rows, col])
+                return acc + (small + both[:count])
+
+            acc = lax.fori_loop(0, width // depth, deepen, jnp.zeros((count, block), jnp.float32))
+            part[s, :, ex_rows] = acc
+            for k in range(1, n_co):
+                part_copy(k, s, b).start()
+            return c
+
+        lax.fori_loop(0, blocks, block_scores, 0)
+
+    def step(t, c):
+        @pl.when(t > 0)
+        def _():
+            relay(t)
 
         s = t - (half - 1)
 
@@ -344,7 +353,7 @@
     local_ids = example_ids - lax.axis_index("ex") * examples
     place = (local_ids[:, None] == lax.iota(jnp.int32, examples)[None, :]).astype(f32)
     return lax.dot_general(
-        normed, place, (((1,), (0,)), ((), ())), precision=lax.Precision.HIGHEST, preferred_element_type=f32
+        normed, place, (((1,), (0,)), ((), ())), precision=lax.Precision.HIGH, preferred_element_type=f32
     )
 
 

time: 181 us -> 181 us (level)
  no operation moved by 1% of the time
where the time goes in v3:
time: 181 us; the launch traced here: 180 us
  Pallas kernels  174 us (96%)
  matrix products  3.88 us (2%)
  other arithmetic  2.35 us (1%)
    pallas_call x1, Pallas kernels, shards(): pl.pallas_call(functools.partial(kernel, n_ex, n_co, pieces), out_shape=(...  174 us
    dot_general x1, matrix products, shards(): lax.dot_general(normed, place, (((1,), (0,)), ((), ())), precision=lax.Pr...  3.88 us

profile of v3, /device:TPU:0, one launch (start us, length us, event | category | flops | bytes accessed | tf_op | source)
XLA Modules:
  0.0 180.1 jit_solution(3265582864541864781)
XLA Ops:
  0.0 0.9 select_reduce_fusion.1
  0.9 0.8 select_reduce_fusion
  1.7 173.8 %shard_map.55 = (f32[256,1024]{1,0:T(8,128)}, f32[8,8,16,8192]{3,2,1,0:T(8,128)}) custom-call(f32[128,8192]{1,0:T(8,128)} %q_ref.1, f32[1024,8192]{1,0:T(8,128)} %g_ref.1, f32[1,8192]{1,0:T(1,128)} %bitcast.2), custom_call_target="tpu_custom_call" | custom-call | tf_op jit(solution)/shard_map/pallas_call | solution.py:316
  175.5 0.7 broadcast_subtract_fusion
  176.2 3.9 %fusion = f32[256,1024]{1,0:T(8,128)} fusion(f32[256,1024]{1,0:T(8,128)} %get-tuple-element.6, s32[1024]{0:T(1024)S(1)} %broadcast_subtract_fusion), kind=kOutput, calls=%fused_computation.1 | convolution fusion | flops 1611661312 | bytes 2101248 | tf_op jit(solution)/shard_map/dot_general | solution.py:355
  (1 shorter events, 0.0 us)
